TPU v7x, 128 devices: a whole 4x4x4 slice. The times are simulated.
128 devices in a mesh: dp: 2 (over x_lo), ctx: 16 (over z, x_hi, core), space: 4 (over y).
Axes of the slice: x: 4 (x_hi: 2, x_lo: 2; x = x_hi * 2 + x_lo), y: 4, z: 4, core: 2. Of those that a mesh axis runs over, the one named last changes fastest.
Arguments:
- inputs: bfloat16 [8, 16, 256, 3072], P('dp', 'ctx', 'space'), may hold values from -64 to 64
- upstream: bfloat16 [8, 16, 256, 3072], P('dp', 'ctx', 'space'), may hold values from -6 to 6
- qkv_weight: bfloat16 [3, 3072, 1536], P(None, None, 'space'), may hold values from -0.109375 to 0.109375
- out_weight: bfloat16 [3072, 1536], P(None, 'space'), may hold values from -0.15625 to 0.15625
Outputs:
- input_grad: bfloat16 [8, 16, 256, 3072], P('dp', 'ctx', 'space')
- qkv_grad: float32 [3, 3072, 1536], P(None, ('dp', 'ctx'), 'space')
- proj_grad: float32 [3072, 1536], P(('dp', 'ctx'), 'space')
All inputs are finite; a program needn't handle non-finite values.
Results may differ from a plain program's by a relative error of at most 0.01.
The roundings to bfloat16 on the way count: a program that leaves them out, or rounds other values in their place, can miss the bound.
Values may be sent and summed in bfloat16 or wider, within the bound.
A program may use at most 192 MiB of HBM per device.

v0:
```python
import math

import jax
import jax.numpy as jnp
from jax import lax
from jax.experimental import pallas as pl
from jax.experimental.pallas import tpu as pltpu
from jax.sharding import PartitionSpec as P

HS = 128
F32 = jnp.float32
BF16 = jnp.bfloat16


def nn(a, b):
    return lax.dot_general(a, b, (((1,), (0,)), ((), ())), preferred_element_type=F32)


def nt(a, b):
    return lax.dot_general(a, b, (((1,), (1,)), ((), ())), preferred_element_type=F32)


def tn(a, b):
    return lax.dot_general(a, b, (((0,), (0,)), ((), ())), preferred_element_type=F32)


def attend_heads(pairs, slot, mine, qkv_ref, front_ref, att_ref, dqkv_ref):
    tokens, width = front_ref.shape
    scale = 1.0 / math.sqrt(HS)
    row = lax.broadcasted_iota(jnp.int32, (tokens, tokens), 0)
    col = lax.broadcasted_iota(jnp.int32, (tokens, tokens), 1)
    valid = (row >= col) & (row % pairs == col % pairs)
    for head in range(width // HS):
        cols = slice(head * HS, (head + 1) * HS)
        k_cols = slice(width + head * HS, width + (head + 1) * HS)
        v_cols = slice(2 * width + head * HS, 2 * width + (head + 1) * HS)
        query, key, value = (qkv_ref[slot, s, :, cols] for s in range(3))
        front = front_ref[:, cols]
        masked = jnp.where(valid, nt(query, key) * scale, F32(-1e30))
        top = jnp.max(masked, axis=-1, keepdims=True)
        expo = jnp.where(valid, jnp.exp(masked - top), F32(0.0))
        probs = expo / jnp.sum(expo, axis=-1, keepdims=True)
        probs_b = probs.astype(BF16)
        att_ref[mine, cols] = nn(probs_b, value).astype(BF16)
        dprobs = nt(front, value)
        dqkv_ref[mine, v_cols] = tn(probs_b, front).astype(BF16)
        weighed = probs * dprobs
        dscore = probs * (dprobs - jnp.sum(weighed, axis=-1, keepdims=True))
        dscore_b = dscore.astype(BF16)
        dqkv_ref[mine, cols] = (nn(dscore_b, key) * scale).astype(BF16)
        dqkv_ref[mine, k_cols] = (tn(dscore_b, query) * scale).astype(BF16)


FORWARD_A, FULL_A, FORWARD_B, FULL_B, LAST_A, LAST_B = 16, 24, 32, 40, 48, 51
COPIES = 54
RANK = {2: 0, 3: 1, 1: 2, 0: 3}


def whole_kernel(n_ctx, n_space, rows, *refs):
    given, (weight_ref, out_weight_ref) = refs[0:2], refs[2:4]
    input_ref, qkv_ref, proj_ref = refs[4:7]
    x_all, u_all, w_all, qkv_two, front, d_all, t_all, part_all, landed = refs[7:16]
    keep_a, keep_b, send_a, send_b, got_a, got_b, fwd_a, fwd_b, full_a, full_b, last_a, last_b = refs[16:28]
    load_sem, swap_send, swap_recv, ring_send, ring_recv = refs[28:33]
    send_sem, recv_sem, back_send, back_recv, out_send, out_recv = refs[33:]
    every = (x_all, u_all)
    tokens, model = given[0].shape
    width = out_weight_ref.shape[1]
    pairs = tokens // n_ctx
    frames = n_ctx // 4
    halved = tokens // 2
    half = rows // 2
    dp, ctx, space = (lax.axis_index(name) for name in ("dp", "ctx", "space"))
    x, z, core = (ctx // 2 % 2) * 2 + dp, ctx // 4, ctx % 2

    def peer(dx, dz, dcore):
        px, pz, pc = (x + dx) % 4, (z + dz) % 4, (core + dcore) % 2
        return (px % 2, (pz * 2 + px // 2) * 2 + pc, space)

    def frame_rows(first, count=1):
        return pl.ds(pl.multiple_of(first * pairs, pairs), count * pairs)

    def unit_rows(unit):
        return pl.ds(pl.multiple_of(unit * tokens, tokens), tokens)

    loads = [
        pltpu.make_async_copy(weight_ref, w_all.at[pl.ds(0, 3)], load_sem.at[0]),
        pltpu.make_async_copy(out_weight_ref, w_all.at[3], load_sem.at[1]),
    ]
    for a in range(2):
        mine = frame_rows(ctx)
        loads.append(pltpu.make_async_copy(given[a].at[mine], every[a].at[mine], load_sem.at[2 + a]))
    for load in loads:
        load.start()

    def signal(to):
        pl.semaphore_signal(
            pltpu.get_barrier_semaphore(), inc=1, device_id=to, device_id_type=pl.DeviceIdType.MESH
        )

    def greet(r, carry):
        signal((dp, (ctx + r) % n_ctx, space))
        return carry

    lax.fori_loop(1, n_ctx, greet, 0)
    for d in range(1, n_space):
        signal((dp, ctx, (space + d) % n_space))
    for d in (1, 3):
        signal(peer(d, 0, 0))
    pl.semaphore_wait(pltpu.get_barrier_semaphore(), n_ctx - 1 + n_space - 1 + 2)

    def send(source, target, send_at, recv_at, to):
        return pltpu.make_async_remote_copy(
            src_ref=source,
            dst_ref=target,
            send_sem=send_at,
            recv_sem=recv_at,
            device_id=to,
            device_id_type=pl.DeviceIdType.MESH,
        )

    def swap(a, r):
        to = (ctx + r) % n_ctx
        return send(
            given[a].at[frame_rows(to)],
            every[a].at[frame_rows(ctx)],
            swap_send.at[a, r],
            swap_recv.at[a, r],
            (dp, to, space),
        )

    def arrival(a, r):
        frm = (ctx + n_ctx - r) % n_ctx
        return send(
            given[a].at[frame_rows(frm)],
            every[a].at[frame_rows(frm)],
            swap_send.at[a, r],
            swap_recv.at[a, r],
            (dp, frm, space),
        )

    def beside(way):
        return (dp, ctx, (space + 1 + 2 * way) % n_space)

    def near(a, h, way):
        at = a * 6 + h * 2 + way
        return send(
            every[a].at[pl.ds(h * halved, halved)],
            every[a].at[pl.ds((1 + way) * tokens + h * halved, halved)],
            ring_send.at[at],
            ring_recv.at[at],
            beside(way),
        )

    def onward(a, way):
        at = a * 6 + 4 + way
        return send(
            every[a].at[pl.ds((1 + way) * tokens + way * halved, halved)],
            every[a].at[pl.ds(3 * tokens + way * halved, halved)],
            ring_send.at[at],
            ring_recv.at[at],
            beside(way),
        )

    for a in range(2):

        def begin(r, carry, a=a):
            swap(a, r).start()
            return carry

        lax.fori_loop(1, n_ctx, begin, 0)

    def spread(a):
        loads[2 + a].wait()
        for h in range(2):

            def settle(frame, carry, a=a):
                r = (ctx + n_ctx - frame) % n_ctx

                @pl.when(r > 0)
                def _():
                    arrival(a, r).wait_recv()

                return carry

            lax.fori_loop(h * n_ctx // 2, (h + 1) * n_ctx // 2, settle, 0)
            for way in range(2):
                near(a, h, way).start()

    def receive(a):
        for way in range(2):
            near(a, way, way).wait_recv()
            onward(a, way).start()
        for way in range(2):
            near(a, 1 - way, way).wait_recv()

    def group(q):
        return (z + 1 + q) % 4 * frames

    def back(q, which):
        part = frame_rows(group(q), frames)
        return send(
            part_all.at[1 + which, part],
            landed.at[which, part],
            back_send.at[q, which],
            back_recv.at[q, which],
            (dp, ctx, (space + (3, 1, 2)[which]) % n_space),
        )

    def outward(frame):
        return send(
            part_all.at[0, frame_rows(frame)],
            input_ref.at[frame_rows(ctx)],
            out_send.at[frame],
            out_recv.at[ctx],
            (dp, frame, space),
        )

    def inward(frame):
        return send(
            part_all.at[0, frame_rows(frame)],
            input_ref.at[frame_rows(frame)],
            out_send.at[frame],
            out_recv.at[frame],
            (dp, frame, space),
        )

    def kept():
        at = frame_rows(ctx)
        return pltpu.make_async_copy(part_all.at[0, at], input_ref.at[at], load_sem.at[4])

    def quarter(q):
        for which in range(3):
            back(q, which).wait_recv()

        def one(i, carry):
            frame = group(q) + i
            at = frame_rows(frame)
            total = part_all[0, at].astype(F32)
            for which in range(3):
                total += landed[which, at].astype(F32)
            part_all[0, at] = total.astype(BF16)

            @pl.when(frame == ctx)
            def _():
                kept().start()

            @pl.when(frame != ctx)
            def _():
                outward(frame).start()

            return carry

        lax.fori_loop(0, frames, one, 0)

    def project(unit):
        def one(s, carry):
            qkv_two[unit % 2, s] = nn(x_all[unit_rows(unit)], w_all[s]).astype(BF16)
            return carry

        lax.fori_loop(0, 3, one, 0)

    def finish(unit):
        mine = unit_rows(unit)
        front[...] = nn(u_all[mine], w_all[3]).astype(BF16)
        attend_heads(pairs, unit % 2, mine, qkv_two, front, t_all, d_all)
        block = model // 6

        def columns(c, carry):
            at = pl.ds(pl.multiple_of(c * block, block), block)
            total = nt(d_all[mine, 0:width], w_all[0, at, :])
            total += nt(d_all[mine, width : 2 * width], w_all[1, at, :])
            total += nt(d_all[mine, 2 * width :], w_all[2, at, :])
            part_all[unit, :, at] = total.astype(BF16)
            return carry

        lax.fori_loop(0, 6, columns, 0)
        for which in range(3):

            @pl.when(unit == 1 + which)
            def _(which=which):
                for q in range(4):
                    back(q, which).start()

    def step(s, carry):
        pace = (s // 2 + 1) // 2
        unit = pace + (pace % 2) * (s % 2) + pace // 2
        first = (s == 0) | (s == 2) | (s == 3) | (s == 6)

        @pl.when(s == 0)
        def _():
            spread(0)
            loads[0].wait()
            loads[1].wait()

        @pl.when(s == 1)
        def _():
            spread(1)

        @pl.when(s == 2)
        def _():
            receive(0)

        @pl.when(s == 4)
        def _():
            receive(1)

        @pl.when(s == 6)
        def _():
            for way in range(2):
                onward(0, way).wait_recv()

        @pl.when(s == 7)
        def _():
            for way in range(2):
                onward(1, way).wait_recv()

        @pl.when(first)
        def _():
            project(unit)

        @pl.when(jnp.logical_not(first))
        def _():
            finish(unit)

        return carry

    lax.fori_loop(0, 8, step, 0)

    def copy(source, target, at, to):
        return send(source, target, send_sem.at[at], recv_sem.at[at], to)

    def far(t):
        k = t // 2
        return t % 2, (2 + k + (k // 2) * (1 + 2 * (k % 2))) % 4

    def trades(t):
        return (
            copy(send_a.at[t % 2], got_a.at[t % 4], 2 * t, peer(0, 0, 1)),
            copy(send_b.at[t % 2], got_b.at[t % 4], 2 * t + 1, peer(0, 0, 1)),
        )

    def forward_a(t, dz, way):
        piece = keep_a.at[t, 1, pl.ds(way * half, half)]
        return copy(piece, fwd_a.at[way, dz], FORWARD_A + 2 * dz + way, peer(1 + 2 * way, 0, 0))

    def full_of_a(t, dz, way):
        return copy(keep_a.at[t, way], full_a.at[way, dz], FULL_A + 2 * dz + way, peer(1 + 2 * way, 0, 0))

    def forward_b(t, dx, hi, way):
        piece = keep_b.at[t, hi, pl.ds(way * half, half)]
        return copy(piece, fwd_b.at[way, dx], FORWARD_B + 2 * dx + way, peer(0, 1 + 2 * way, 0))

    def full_of_b(t, dx, hi, way):
        return copy(keep_b.at[t, hi], full_b.at[way, dx], FULL_B + 2 * dx + way, peer(0, 1 + 2 * way, 0))

    def compute(t):
        p, dz = far(t)
        start = ((x + p) % 4) // 2
        off = 4 * rows * (((dp + p) % 2) * 4 + (z + dz) % 4)
        columns = pl.ds(pl.multiple_of(off, 128), 4 * rows)

        @pl.when(t >= 2)
        def _():
            for trade in trades(t - 2):
                trade.wait_send()

        def put(send_ref, keep_ref, low, total):
            high = low + total.shape[1]
            for hi in range(2):
                spot = (hi + 2 - start) % 2
                even = total[2 * hi * rows : (2 * hi + 1) * rows]
                odd = total[(2 * hi + 1) * rows : (2 * hi + 2) * rows]

                @pl.when(core == 0)
                def _():
                    keep_ref[t, spot, :, low:high] = even
                    send_ref[t % 2, spot, :, low:high] = odd

                @pl.when(core == 1)
                def _():
                    keep_ref[t, spot, :, low:high] = odd
                    send_ref[t % 2, spot, :, low:high] = even

        source = x_all[:, columns]
        put(send_a, keep_a, 0, tn(source, d_all[:, : 2 * width]))
        put(send_b, keep_b, 0, tn(source, d_all[:, 2 * width :]))
        put(send_b, keep_b, width, tn(u_all[:, columns], t_all[...]))
        for trade in trades(t):
            trade.start()

    def pair_up(t):
        p, dz = far(t)
        for trade in trades(t):
            trade.wait_recv()
        keep_a[t] += got_a[t % 4]
        keep_b[t] += got_b[t % 4]

        @pl.when(p == 0)
        def _():
            for way in range(2):
                forward_a(t, dz, way).start()

        @pl.when(dz == 2)
        def _():
            for hi in range(2):
                for way in range(2):
                    forward_b(t, p + 2 * hi, hi, way).start()

    def pass_on(t):
        p, dz = far(t)

        @pl.when(p == 1)
        def _():
            for way in range(2):
                forward_a(t, dz, way).wait_recv()
                keep_a[t, way, pl.ds(way * half, half)] += fwd_a[way, dz]
                full_of_a(t, dz, way).start()

        @pl.when(dz % 2 == 1)
        def _():
            way = dz // 2
            for hi in range(2):
                dx = p + 2 * hi
                forward_b(t, dx, hi, way).wait_recv()
                part = pl.ds(pl.multiple_of(way * half, half), half)
                keep_b[t, hi, part] += fwd_b[way, dx]
                full_of_b(t, dx, hi, way).start()

    def work(t, carry):
        @pl.when(t < 8)
        def _():
            compute(t)

        @pl.when((t >= 1) & (t < 9))
        def _():
            pair_up(t - 1)

        @pl.when(t >= 2)
        def _():
            pass_on(t - 2)

        return carry

    lax.fori_loop(0, 10, work, 0)

    def finish_a(dz):
        t = 2 * RANK[dz]
        for way in range(2):
            full_of_a(t, dz, way).wait_recv()
        keep_a[t, 0] += full_a[0, dz] + full_a[1, dz]

    def finish_b(dx):
        t, hi = 6 + dx % 2, dx // 2
        for way in range(2):
            full_of_b(t, dx, hi, way).wait_recv()
        keep_b[t, hi] += full_b[0, dx] + full_b[1, dx]

    def last_of_a(dz):
        return copy(keep_a.at[2 * RANK[dz], 0], last_a.at[dz - 1], LAST_A + dz - 1, peer(0, dz, 0))

    def last_of_b(dx):
        return copy(keep_b.at[6 + dx % 2, dx // 2], last_b.at[dx - 1], LAST_B + dx - 1, peer(dx, 0, 0))

    quarter(0)
    quarter(1)
    for d in (2, 3, 1):
        finish_a(d)
        last_of_a(d).start()
        finish_b(d)
        last_of_b(d).start()
    finish_a(0)
    finish_b(0)
    quarter(2)
    for d in (2, 3, 1):
        last_of_a(d).wait_recv()
        last_of_b(d).wait_recv()
    sum_a = keep_a[6, 0] + last_a[0] + last_a[1] + last_a[2]
    sum_b = keep_b[6, 0] + last_b[0] + last_b[1] + last_b[2]
    qkv_ref[0] = sum_a[:, :width]
    qkv_ref[1] = sum_a[:, width:]
    qkv_ref[2] = sum_b[:, :width]
    proj_ref[...] = sum_b[:, width:]
    quarter(3)

    def settle(frame, carry):
        @pl.when(frame == ctx)
        def _():
            kept().wait()

        @pl.when(frame != ctx)
        def _():
            outward(frame).wait_send()
            inward(frame).wait_recv()

        return carry

    lax.fori_loop(0, n_ctx, settle, 0)

    def home(q, carry):
        for which in range(3):
            back(q, which).wait_send()
        return carry

    lax.fori_loop(0, 4, home, 0)
    for a in range(2):

        def sent(r, carry, a=a):
            swap(a, r).wait_send()
            return carry

        lax.fori_loop(1, n_ctx, sent, 0)
        for way in range(2):
            for h in range(2):
                near(a, h, way).wait_send()
            onward(a, way).wait_send()
    for t in (6, 7):
        for trade in trades(t):
            trade.wait_send()

    def drain(t, carry):
        p, dz = far(t)

        @pl.when(p == 0)
        def _():
            for way in range(2):
                forward_a(t, dz, way).wait_send()

        @pl.when(p == 1)
        def _():
            for way in range(2):
                full_of_a(t, dz, way).wait_send()

        @pl.when(dz == 2)
        def _():
            for hi in range(2):
                for way in range(2):
                    forward_b(t, p + 2 * hi, hi, way).wait_send()

        @pl.when(dz % 2 == 1)
        def _():
            for hi in range(2):
                full_of_b(t, p + 2 * hi, hi, dz // 2).wait_send()

        return carry

    lax.fori_loop(0, 8, drain, 0)
    for d in (2, 3, 1):
        last_of_a(d).wait_send()
        last_of_b(d).wait_send()


def whole(n_ctx, n_space, rows, inputs, upstream, qkv_weight, out_weight):
    tokens, model = inputs.shape
    width = out_weight.shape[1]
    wide = 2 * width
    vmem, dma = pltpu.VMEM, pltpu.SemaphoreType.DMA
    return pl.pallas_call(
        lambda *refs: whole_kernel(n_ctx, n_space, rows, *refs),
        out_shape=(
            jax.ShapeDtypeStruct((tokens, model), BF16),
            jax.ShapeDtypeStruct((3, rows, width), F32),
            jax.ShapeDtypeStruct((rows, width), F32),
        ),
        in_specs=[pl.BlockSpec(memory_space=pl.ANY)] * 4,
        out_specs=(pl.BlockSpec(memory_space=pl.ANY),) + (pl.BlockSpec(memory_space=vmem),) * 2,
        scratch_shapes=[
            vmem((4 * tokens, model), BF16),
            vmem((4 * tokens, model), BF16),
            vmem((4, model, width), BF16),
            vmem((2, 3, tokens, width), BF16),
            vmem((tokens, width), BF16),
            vmem((4 * tokens, 3 * width), BF16),
            vmem((4 * tokens, width), BF16),
            vmem((4, tokens, model), BF16),
            vmem((3, tokens, model), BF16),
            vmem((8, 2, rows, wide), F32),
            vmem((8, 2, rows, wide), F32),
            vmem((2, 2, rows, wide), F32),
            vmem((2, 2, rows, wide), F32),
            vmem((4, 2, rows, wide), F32),
            vmem((4, 2, rows, wide), F32),
            vmem((2, 4, rows // 2, wide), F32),
            vmem((2, 4, rows // 2, wide), F32),
            vmem((2, 4, rows, wide), F32),
            vmem((2, 4, rows, wide), F32),
            vmem((3, rows, wide), F32),
            vmem((3, rows, wide), F32),
            dma((5,)),
            dma((2, n_ctx)),
            dma((2, n_ctx)),
            dma((12,)),
            dma((12,)),
            dma((COPIES,)),
            dma((COPIES,)),
            dma((4, 3)),
            dma((4, 3)),
            dma((n_ctx,)),
            dma((n_ctx,)),
        ],
        compiler_params=pltpu.CompilerParams(
            collective_id=0, has_side_effects=True, vmem_limit_bytes=67043328
        ),
        name="whole",
    )(inputs, upstream, qkv_weight, out_weight)


def solution(mesh):
    n_dp, n_ctx, n_space = mesh.shape["dp"], mesh.shape["ctx"], mesh.shape["space"]

    def body(inputs, upstream, qkv_weight, out_weight):
        clips, single, patches, model = inputs.shape
        tokens = clips * patches
        input_grad, qkv_grad, proj_grad = whole(
            n_ctx,
            n_space,
            model // (n_dp * n_ctx),
            inputs.reshape(tokens, model),
            upstream.reshape(tokens, model),
            qkv_weight,
            out_weight,
        )
        return input_grad.reshape(clips, single, patches, model), qkv_grad, proj_grad

    placed = (
        P("dp", "ctx", "space", None),
        P("dp", "ctx", "space", None),
        P(None, None, "space"),
        P(None, "space"),
    )
    return jax.shard_map(
        body,
        mesh=mesh,
        in_specs=placed,
        out_specs=(
            P("dp", "ctx", "space", None),
            P(None, ("dp", "ctx"), "space"),
            P(("dp", "ctx"), "space"),
        ),
        check_vma=False,
    )
```

profile of v0, /device:TPU:1, one launch (start us, length us, event | category | flops | bytes accessed | tf_op | source)
XLA Modules:
  0.0 234.3 jit_solution(2202600325777320785)
XLA Ops:
  0.6 229.5 %whole.1 = (bf16[256,3072]{1,0:T(8,128)(2,1)}, f32[3,96,384]{2,1,0:T(8,128)}, f32[96,384]{1,0:T(8,128)}) custom-call(bf16[256,3072]{1,0:T(8,128)(2,1)} %bitcast.5, bf16[256,3072]{1,0:T(8,128)(2,1)} %bitcast.6, bf16[3,3072,384]{2,1,0:T(8,128)(2,1)} %refs_2_.1, bf16[3072,384]{1,0:T(8,128)(2,1)} %refs_3_.1), custom_call_target="tpu_custom_call" | custom-call | tf_op jit(solution)/shard_map/whole/pallas_call | solution.py:558
  230.1 0.0 copy-start
  230.1 0.0 copy-start.1
  230.1 2.7 %copy.11 = bf16[4,1,64,3072]{3,2,1,0:T(8,128)(2,1)} copy(bf16[4,1,64,3072]{3,2,1,0:T(8,128)(2,1)} %bitcast.7) | data formatting | bytes 3145728
  232.9 0.0 copy-done
  232.9 0.8 copy.12
  233.6 0.0 copy-done.1
  233.6 0.7 copy.13
Async XLA Ops:
  230.1 2.7 %copy-start = (f32[3,96,384]{2,1,0:T(8,128)S(1)}, f32[3,96,384]{2,1,0:T(8,128)}, u32[]{:S(2)}) copy-start(f32[3,96,384]{2,1,0:T(8,128)} %get-tuple-element.16) | copy-start | bytes 1327108
  230.1 3.5 %copy-start.1 = (f32[96,384]{1,0:T(8,128)S(1)}, f32[96,384]{1,0:T(8,128)}, u32[]{:S(2)}) copy-start(f32[96,384]{1,0:T(8,128)} %get-tuple-element.17) | copy-start | bytes 442372
where the time goes:
time: 234 us
  Pallas kernels  229 us (98%)
  local copies, waits for them, and re-layouts  4.14 us (2%)
    pallas_call x1, Pallas kernels, whole(): pl.pallas_call(lambda *refs: whole_kernel(n_ctx, n_space, rows, *refs), o...  229 us

commit v1 on v0

--- a/solution.py
+++ b/solution.py
@@ -59,16 +59,18 @@
 def whole_kernel(n_ctx, n_space, rows, *refs):
     given, (weight_ref, out_weight_ref) = refs[0:2], refs[2:4]
     input_ref, qkv_ref, proj_ref = refs[4:7]
-    x_all, u_all, w_all, qkv_two, front, d_all, t_all, part_all, landed = refs[7:16]
-    keep_a, keep_b, send_a, send_b, got_a, got_b, fwd_a, fwd_b, full_a, full_b, last_a, last_b = refs[16:28]
-    load_sem, swap_send, swap_recv, ring_send, ring_recv = refs[28:33]
-    send_sem, recv_sem, back_send, back_recv, out_send, out_recv = refs[33:]
+    x_all, u_all, w_all, qkv_two, front, d_all, t_all, part_all, landed, early = refs[7:17]
+    keep_a, keep_b, send_a, send_b, got_a, got_b, fwd_a, fwd_b, full_a, full_b, last_a, last_b = refs[17:29]
+    load_sem, swap_send, swap_recv, ring_send, ring_recv = refs[29:34]
+    send_sem, recv_sem, back_send, back_recv, out_send, out_recv = refs[34:40]
+    early_send, early_recv, pass_send, pass_recv = refs[40:]
     every = (x_all, u_all)
     tokens, model = given[0].shape
     width = out_weight_ref.shape[1]
     pairs = tokens // n_ctx
     frames = n_ctx // 4
     halved = tokens // 2
+    some = early.shape[2]
     half = rows // 2
     dp, ctx, space = (lax.axis_index(name) for name in ("dp", "ctx", "space"))
     x, z, core = (ctx // 2 % 2) * 2 + dp, ctx // 4, ctx % 2
@@ -142,11 +144,48 @@
     def beside(way):
         return (dp, ctx, (space + 1 + 2 * way) % n_space)
 
+    def ahead_of_all(way):
+        return send(
+            given[1].at[:, pl.ds(0, some)],
+            early.at[way],
+            early_send.at[way],
+            early_recv.at[way],
+            beside(way),
+        )
+
+    def passing(way, r):
+        to = (ctx + r) % n_ctx
+        return send(
+            early.at[way, frame_rows(to)],
+            u_all.at[frame_rows((1 + way) * n_ctx + ctx), pl.ds(0, some)],
+            pass_send.at[way, r],
+            pass_recv.at[way, r],
+            (dp, to, space),
+        )
+
+    def passed(way, r):
+        frm = (ctx + n_ctx - r) % n_ctx
+        return send(
+            early.at[way, frame_rows(frm)],
+            u_all.at[frame_rows((1 + way) * n_ctx + frm), pl.ds(0, some)],
+            pass_send.at[way, r],
+            pass_recv.at[way, r],
+            (dp, frm, space),
+        )
+
+    def unpassed(way):
+        return pltpu.make_async_copy(
+            early.at[way, frame_rows(ctx)],
+            u_all.at[frame_rows((1 + way) * n_ctx + ctx), pl.ds(0, some)],
+            load_sem.at[5 + way],
+        )
+
     def near(a, h, way):
         at = a * 6 + h * 2 + way
-        return send(
-            every[a].at[pl.ds(h * halved, halved)],
-            every[a].at[pl.ds((1 + way) * tokens + h * halved, halved)],
+        low = a * some
+        return send(
+            every[a].at[pl.ds(h * halved, halved), pl.ds(low, model - low)],
+            every[a].at[pl.ds((1 + way) * tokens + h * halved, halved), pl.ds(low, model - low)],
             ring_send.at[at],
             ring_recv.at[at],
             beside(way),
@@ -162,6 +201,8 @@
             beside(way),
         )
 
+    for way in range(2):
+        ahead_of_all(way).start()
     for a in range(2):
 
         def begin(r, carry, a=a):
@@ -186,6 +227,27 @@
             lax.fori_loop(h * n_ctx // 2, (h + 1) * n_ctx // 2, settle, 0)
             for way in range(2):
                 near(a, h, way).start()
+
+    def pass_all():
+        for way in range(2):
+            ahead_of_all(way).wait_recv()
+            unpassed(way).start()
+
+            def one(r, carry, way=way):
+                passing(way, r).start()
+                return carry
+
+            lax.fori_loop(1, n_ctx, one, 0)
+
+    def all_passed():
+        for way in range(2):
+            unpassed(way).wait()
+
+            def one(r, carry, way=way):
+                passed(way, r).wait_recv()
+                return carry
+
+            lax.fori_loop(1, n_ctx, one, 0)
 
     def receive(a):
         for way in range(2):
@@ -290,6 +352,7 @@
         @pl.when(s == 0)
         def _():
             spread(0)
+            pass_all()
             loads[0].wait()
             loads[1].wait()
 
@@ -303,6 +366,7 @@
 
         @pl.when(s == 4)
         def _():
+            all_passed()
             receive(1)
 
         @pl.when(s == 6)
@@ -463,7 +527,6 @@
         return copy(keep_b.at[6 + dx % 2, dx // 2], last_b.at[dx - 1], LAST_B + dx - 1, peer(dx, 0, 0))
 
     quarter(0)
-    quarter(1)
     for d in (2, 3, 1):
         finish_a(d)
         last_of_a(d).start()
@@ -471,6 +534,7 @@
         last_of_b(d).start()
     finish_a(0)
     finish_b(0)
+    quarter(1)
     quarter(2)
     for d in (2, 3, 1):
         last_of_a(d).wait_recv()
@@ -514,6 +578,14 @@
             for h in range(2):
                 near(a, h, way).wait_send()
             onward(a, way).wait_send()
+    for way in range(2):
+        ahead_of_all(way).wait_send()
+
+        def gone(r, carry, way=way):
+            passing(way, r).wait_send()
+            return carry
+
+        lax.fori_loop(1, n_ctx, gone, 0)
     for t in (6, 7):
         for trade in trades(t):
             trade.wait_send()
@@ -574,6 +646,7 @@
             vmem((4 * tokens, width), BF16),
             vmem((4, tokens, model), BF16),
             vmem((3, tokens, model), BF16),
+            vmem((2, tokens, model // 2), BF16),
             vmem((8, 2, rows, wide), F32),
             vmem((8, 2, rows, wide), F32),
             vmem((2, 2, rows, wide), F32),
@@ -586,7 +659,7 @@
             vmem((2, 4, rows, wide), F32),
             vmem((3, rows, wide), F32),
             vmem((3, rows, wide), F32),
-            dma((5,)),
+            dma((7,)),
             dma((2, n_ctx)),
             dma((2, n_ctx)),
             dma((12,)),
@@ -597,6 +670,10 @@
             dma((4, 3)),
             dma((n_ctx,)),
             dma((n_ctx,)),
+            dma((2,)),
+            dma((2,)),
+            dma((2, n_ctx)),
+            dma((2, n_ctx)),
         ],
         compiler_params=pltpu.CompilerParams(
             collective_id=0, has_side_effects=True, vmem_limit_bytes=67043328

time: 234 us -> 214 us (0.915)
  Pallas kernels: 229 us -> 209 us
    pallas_call x1, Pallas kernels: 229 us -> 209 us  [whole(): pl.pallas_call(lambda *refs: whole_kernel(n_ctx, n_space, rows, *refs), o...]
where the time goes in v1:
time: 214 us
  Pallas kernels  209 us (98%)
  local copies, waits for them, and re-layouts  4.14 us (2%)
    pallas_call x1, Pallas kernels, whole(): pl.pallas_call(lambda *refs: whole_kernel(n_ctx, n_space, rows, *refs), o...  209 us

profile of v1, /device:TPU:1, one launch (start us, length us, event | category | flops | bytes accessed | tf_op | source)
XLA Modules:
  0.0 214.1 jit_solution(10675660489573010122)
XLA Ops:
  0.6 209.3 %whole.1 = (bf16[256,3072]{1,0:T(8,128)(2,1)}, f32[3,96,384]{2,1,0:T(8,128)}, f32[96,384]{1,0:T(8,128)}) custom-call(bf16[256,3072]{1,0:T(8,128)(2,1)} %bitcast.5, bf16[256,3072]{1,0:T(8,128)(2,1)} %bitcast.6, bf16[3,3072,384]{2,1,0:T(8,128)(2,1)} %refs_2_.1, bf16[3072,384]{1,0:T(8,128)(2,1)} %refs_3_.1), custom_call_target="tpu_custom_call" | custom-call | tf_op jit(solution)/shard_map/whole/pallas_call | solution.py:630
  210.0 0.0 copy-start
  210.0 0.0 copy-start.1
  210.0 2.7 %copy.11 = bf16[4,1,64,3072]{3,2,1,0:T(8,128)(2,1)} copy(bf16[4,1,64,3072]{3,2,1,0:T(8,128)(2,1)} %bitcast.7) | data formatting | bytes 3145728
  212.7 0.0 copy-done
  212.7 0.8 copy.12
  213.5 0.0 copy-done.1
  213.5 0.7 copy.13
Async XLA Ops:
  210.0 2.7 %copy-start = (f32[3,96,384]{2,1,0:T(8,128)S(1)}, f32[3,96,384]{2,1,0:T(8,128)}, u32[]{:S(2)}) copy-start(f32[3,96,384]{2,1,0:T(8,128)} %get-tuple-element.16) | copy-start | bytes 1327108
  210.0 3.5 %copy-start.1 = (f32[96,384]{1,0:T(8,128)S(1)}, f32[96,384]{1,0:T(8,128)}, u32[]{:S(2)}) copy-start(f32[96,384]{1,0:T(8,128)} %get-tuple-element.17) | copy-start | bytes 442372

commit v2 on v1

--- a/solution.py
+++ b/solution.py
@@ -326,6 +326,9 @@
         mine = unit_rows(unit)
         front[...] = nn(u_all[mine], w_all[3]).astype(BF16)
         attend_heads(pairs, unit % 2, mine, qkv_two, front, t_all, d_all)
+
+    def give_back(unit):
+        mine = unit_rows(unit)
         block = model // 6
 
         def columns(c, carry):
@@ -387,6 +390,10 @@
         def _():
             finish(unit)
 
+        @pl.when(jnp.logical_not(first) & (unit < 3))
+        def _():
+            give_back(unit)
+
         return carry
 
     lax.fori_loop(0, 8, step, 0)
@@ -492,6 +499,10 @@
                 full_of_b(t, dx, hi, way).start()
 
     def work(t, carry):
+        @pl.when(t == 1)
+        def _():
+            give_back(3)
+
         @pl.when(t < 8)
         def _():
             compute(t)
@@ -526,7 +537,6 @@
     def last_of_b(dx):
         return copy(keep_b.at[6 + dx % 2, dx // 2], last_b.at[dx - 1], LAST_B + dx - 1, peer(dx, 0, 0))
 
-    quarter(0)
     for d in (2, 3, 1):
         finish_a(d)
         last_of_a(d).start()
@@ -534,6 +544,7 @@
         last_of_b(d).start()
     finish_a(0)
     finish_b(0)
+    quarter(0)
     quarter(1)
     quarter(2)
     for d in (2, 3, 1):

time: 214 us -> 211 us (0.986)
  Pallas kernels: 209 us -> 205 us
    pallas_call x1, Pallas kernels: 209 us -> 205 us  [whole(): pl.pallas_call(lambda *refs: whole_kernel(n_ctx, n_space, rows, *refs), o...]
where the time goes in v2:
time: 211 us; the launch traced here: 209 us
  Pallas kernels  205 us (97%)
  local copies, waits for them, and re-layouts  4.14 us (2%)
    pallas_call x1, Pallas kernels, whole(): pl.pallas_call(lambda *refs: whole_kernel(n_ctx, n_space, rows, *refs), o...  205 us

profile of v2, /device:TPU:1, one launch (start us, length us, event | category | flops | bytes accessed | tf_op | source)
XLA Modules:
  0.0 209.4 jit_solution(2817410200252712346)
XLA Ops:
  0.6 204.6 %whole.1 = (bf16[256,3072]{1,0:T(8,128)(2,1)}, f32[3,96,384]{2,1,0:T(8,128)}, f32[96,384]{1,0:T(8,128)}) custom-call(bf16[256,3072]{1,0:T(8,128)(2,1)} %bitcast.5, bf16[256,3072]{1,0:T(8,128)(2,1)} %bitcast.6, bf16[3,3072,384]{2,1,0:T(8,128)(2,1)} %refs_2_.1, bf16[3072,384]{1,0:T(8,128)(2,1)} %refs_3_.1), custom_call_target="tpu_custom_call" | custom-call | tf_op jit(solution)/shard_map/whole/pallas_call | solution.py:641
  205.2 0.0 copy-start
  205.3 0.0 copy-start.1
  205.3 2.7 %copy.11 = bf16[4,1,64,3072]{3,2,1,0:T(8,128)(2,1)} copy(bf16[4,1,64,3072]{3,2,1,0:T(8,128)(2,1)} %bitcast.7) | data formatting | bytes 3145728
  208.0 0.0 copy-done
  208.0 0.8 copy.12
  208.7 0.0 copy-done.1
  208.7 0.7 copy.13
Async XLA Ops:
  205.2 2.7 %copy-start = (f32[3,96,384]{2,1,0:T(8,128)S(1)}, f32[3,96,384]{2,1,0:T(8,128)}, u32[]{:S(2)}) copy-start(f32[3,96,384]{2,1,0:T(8,128)} %get-tuple-element.16) | copy-start | bytes 1327108
  205.3 3.5 %copy-start.1 = (f32[96,384]{1,0:T(8,128)S(1)}, f32[96,384]{1,0:T(8,128)}, u32[]{:S(2)}) copy-start(f32[96,384]{1,0:T(8,128)} %get-tuple-element.17) | copy-start | bytes 442372

commit v3 on v2

--- a/solution.py
+++ b/solution.py
@@ -24,8 +24,8 @@
     return lax.dot_general(a, b, (((0,), (0,)), ((), ())), preferred_element_type=F32)
 
 
-def attend_heads(pairs, slot, mine, qkv_ref, front_ref, att_ref, dqkv_ref):
-    tokens, width = front_ref.shape
+def attend_heads(pairs, slot, mine, qkv_ref, att_ref, dqkv_ref):
+    tokens, width = qkv_ref.shape[2:]
     scale = 1.0 / math.sqrt(HS)
     row = lax.broadcasted_iota(jnp.int32, (tokens, tokens), 0)
     col = lax.broadcasted_iota(jnp.int32, (tokens, tokens), 1)
@@ -35,7 +35,7 @@
         k_cols = slice(width + head * HS, width + (head + 1) * HS)
         v_cols = slice(2 * width + head * HS, 2 * width + (head + 1) * HS)
         query, key, value = (qkv_ref[slot, s, :, cols] for s in range(3))
-        front = front_ref[:, cols]
+        front = att_ref[mine, cols]
         masked = jnp.where(valid, nt(query, key) * scale, F32(-1e30))
         top = jnp.max(masked, axis=-1, keepdims=True)
         expo = jnp.where(valid, jnp.exp(masked - top), F32(0.0))
@@ -59,11 +59,11 @@
 def whole_kernel(n_ctx, n_space, rows, *refs):
     given, (weight_ref, out_weight_ref) = refs[0:2], refs[2:4]
     input_ref, qkv_ref, proj_ref = refs[4:7]
-    x_all, u_all, w_all, qkv_two, front, d_all, t_all, part_all, landed, early = refs[7:17]
-    keep_a, keep_b, send_a, send_b, got_a, got_b, fwd_a, fwd_b, full_a, full_b, last_a, last_b = refs[17:29]
-    load_sem, swap_send, swap_recv, ring_send, ring_recv = refs[29:34]
-    send_sem, recv_sem, back_send, back_recv, out_send, out_recv = refs[34:40]
-    early_send, early_recv, pass_send, pass_recv = refs[40:]
+    x_all, u_all, w_all, qkv_two, d_all, t_all, part_all, landed, early = refs[7:16]
+    keep_a, keep_b, send_a, send_b, got_a, got_b, fwd_a, fwd_b, full_a, full_b, last_a, last_b = refs[16:28]
+    load_sem, swap_send, swap_recv, ring_send, ring_recv = refs[28:33]
+    send_sem, recv_sem, back_send, back_recv, out_send, out_recv = refs[33:39]
+    early_send, early_recv, pass_send, pass_recv = refs[39:]
     every = (x_all, u_all)
     tokens, model = given[0].shape
     width = out_weight_ref.shape[1]
@@ -324,8 +324,8 @@
 
     def finish(unit):
         mine = unit_rows(unit)
-        front[...] = nn(u_all[mine], w_all[3]).astype(BF16)
-        attend_heads(pairs, unit % 2, mine, qkv_two, front, t_all, d_all)
+        t_all[mine] = nn(u_all[mine], w_all[3]).astype(BF16)
+        attend_heads(pairs, unit % 2, mine, qkv_two, t_all, d_all)
 
     def give_back(unit):
         mine = unit_rows(unit)
@@ -652,12 +652,11 @@
             vmem((4 * tokens, model), BF16),
             vmem((4, model, width), BF16),
             vmem((2, 3, tokens, width), BF16),
-            vmem((tokens, width), BF16),
             vmem((4 * tokens, 3 * width), BF16),
             vmem((4 * tokens, width), BF16),
             vmem((4, tokens, model), BF16),
             vmem((3, tokens, model), BF16),
-            vmem((2, tokens, model // 2), BF16),
+            vmem((2, tokens, model * 13 // 24), BF16),
             vmem((8, 2, rows, wide), F32),
             vmem((8, 2, rows, wide), F32),
             vmem((2, 2, rows, wide), F32),

time: 211 us -> 211 us (level)
  no operation moved by 1% of the time
where the time goes in v3:
time: 211 us; the launch traced here: 208 us
  Pallas kernels  204 us (97%)
  local copies, waits for them, and re-layouts  4.14 us (2%)
    pallas_call x1, Pallas kernels, whole(): pl.pallas_call(lambda *refs: whole_kernel(n_ctx, n_space, rows, *refs), o...  204 us

profile of v3, /device:TPU:1, one launch (start us, length us, event | category | flops | bytes accessed | tf_op | source)
XLA Modules:
  0.0 208.4 jit_solution(11889561000018857754)
XLA Ops:
  0.6 203.6 %whole.1 = (bf16[256,3072]{1,0:T(8,128)(2,1)}, f32[3,96,384]{2,1,0:T(8,128)}, f32[96,384]{1,0:T(8,128)}) custom-call(bf16[256,3072]{1,0:T(8,128)(2,1)} %bitcast.5, bf16[256,3072]{1,0:T(8,128)(2,1)} %bitcast.6, bf16[3,3072,384]{2,1,0:T(8,128)(2,1)} %refs_2_.1, bf16[3072,384]{1,0:T(8,128)(2,1)} %refs_3_.1), custom_call_target="tpu_custom_call" | custom-call | tf_op jit(solution)/shard_map/whole/pallas_call | solution.py:641
  204.3 0.0 copy-start
  204.3 0.0 copy-start.1
  204.3 2.7 %copy.11 = bf16[4,1,64,3072]{3,2,1,0:T(8,128)(2,1)} copy(bf16[4,1,64,3072]{3,2,1,0:T(8,128)(2,1)} %bitcast.7) | data formatting | bytes 3145728
  207.0 0.0 copy-done
  207.0 0.8 copy.12
  207.8 0.0 copy-done.1
  207.8 0.7 copy.13
Async XLA Ops:
  204.3 2.7 %copy-start = (f32[3,96,384]{2,1,0:T(8,128)S(1)}, f32[3,96,384]{2,1,0:T(8,128)}, u32[]{:S(2)}) copy-start(f32[3,96,384]{2,1,0:T(8,128)} %get-tuple-element.16) | copy-start | bytes 1327108
  204.3 3.5 %copy-start.1 = (f32[96,384]{1,0:T(8,128)S(1)}, f32[96,384]{1,0:T(8,128)}, u32[]{:S(2)}) copy-start(f32[96,384]{1,0:T(8,128)} %get-tuple-element.17) | copy-start | bytes 442372
